TPU v7x, 32 devices: a whole 2x2x4 slice. The times are simulated.
32 devices in a mesh: theta: 16 (over z, x, core), gz: 2 (over y).
Axes of the slice: x: 2, y: 2, z: 4, core: 2. Of those that a mesh axis runs over, the one named last changes fastest.
Arguments:
- field: float32 [16, 1024, 1024], P('gz', 'theta'), parts along dimension 0, may hold values from -6 to 6
- courant: float32 [1024], replicated, may hold values from 0.2 to 0.8
Outputs:
- advanced: float32 [16, 1024, 1024], P('gz', 'theta'), parts along dimension 0
There are 2 independent parts, one for each index of `gz`. A program takes and returns all parts, laid end to end along the dimension named above; an argument that names none is the same for every part. Nothing has to cross between parts.
All inputs are finite; a program needn't handle non-finite values.
Results may differ from a plain program's by a relative error of at most 0.00007.
Values sent between devices are 32-bit elements; how exact they have to be, the bound alone decides.
A program may use at most 128 MiB of HBM per device.

v0:
```python
import math

import jax
import jax.numpy as jnp
from jax import lax
from jax.sharding import PartitionSpec as P

stencil_weights = (4.0 / 5.0, -1.0 / 5.0, 4.0 / 105.0, -1.0 / 280.0)
radial_step = 0.2


def shifted(x, axis, by):
    size = lax.axis_size(axis)
    return lax.ppermute(x, axis, [(i, (i + by) % size) for i in range(size)])


def with_halo(x, sides, width):
    for axis, dim in sides:
        size, length = (lax.axis_size(axis), x.shape[dim])
        up = [(i, (i + 1) % size) for i in range(size)]
        down = [(j, i) for i, j in up]
        last = lax.slice_in_dim(x, length - width, length, axis=dim)
        leading = lax.slice_in_dim(x, 0, width, axis=dim)
        before = lax.ppermute(last, axis, up)
        after = lax.ppermute(leading, axis, down)
        x = jnp.concatenate([before, x, after], axis=dim)
    return x


def diameter_blocks(radial_count):
    intervals = 2 * radial_count - 1
    row_index = jnp.arange(radial_count, dtype=jnp.int32)[:, None]
    col_index = jnp.arange(2 * radial_count, dtype=jnp.int32)[None, :]
    angle_unit = math.pi / (2 * intervals)
    summed = (row_index + col_index).astype(jnp.float32) * angle_unit
    differ = (row_index - col_index).astype(jnp.float32) * angle_unit
    spacing = -2.0 * jnp.sin(summed) * jnp.sin(differ)
    same = row_index == col_index
    row_factor = jnp.where(row_index == 0, 2.0, 1.0).astype(jnp.float32)
    col_factor = jnp.where((col_index == 0) | (col_index == intervals), 2.0, 1.0).astype(
        jnp.float32
    )
    parity = jnp.where((row_index + col_index) % 2 == 0, 1.0, -1.0).astype(jnp.float32)
    safe_spacing = jnp.where(same, 1.0, spacing)
    offdiag = jnp.where(same, 0.0, row_factor / col_factor * parity / safe_spacing)
    matrix = offdiag - jnp.where(same, jnp.sum(offdiag, axis=1, keepdims=True), 0.0)
    near = matrix[:, :radial_count].T
    far = matrix[:, radial_count:][:, ::-1].T
    return (near, far)


def radial_weight(radial_count):
    intervals = 2 * radial_count - 1
    angles = jnp.arange(radial_count, dtype=jnp.int32).astype(jnp.float32) * (math.pi / intervals)
    return jnp.sin(angles) ** 2


def azimuth_difference(extended, rows):
    total = jnp.zeros((extended.shape[0], rows, extended.shape[2]), jnp.float32)
    for offset in range(1, 5):
        total = total + stencil_weights[offset - 1] * (
            extended[:, 4 + offset : 4 + offset + rows]
            - extended[:, 4 - offset : 4 - offset + rows]
        )
    return total


def body(field, courant):
    radial_count = field.shape[2]
    near, far = diameter_blocks(radial_count)
    weight = radial_weight(radial_count)
    tau = radial_step / (2 * radial_count - 1)
    cycle_count = lax.axis_size("theta")
    half_cycle = cycle_count // 2

    def opposite_derivative(state):
        own_rows = state.reshape(-1, radial_count)
        local_part = jnp.dot(own_rows, near, precision=lax.Precision.HIGHEST)
        other = shifted(state, "theta", half_cycle)
        total = local_part + jnp.dot(
            other.reshape(-1, radial_count), far, precision=lax.Precision.HIGHEST
        )
        return total.reshape(state.shape)

    def section_rate(extended):
        rows = extended.shape[1] - 8
        state = extended[:, 4 : 4 + rows]
        azimuth = azimuth_difference(extended, rows)
        deriv = opposite_derivative(state)
        return -courant * azimuth - tau * weight * state * deriv

    def widen(state):
        return with_halo(state, (("theta", 1),), 4)

    first = field + section_rate(widen(field))
    second = 0.75 * field + 0.25 * (first + section_rate(widen(first)))
    return field / 3.0 + 2.0 / 3.0 * (second + section_rate(widen(second)))


def solution(mesh):
    placed = (P("gz", "theta", None), P())
    return jax.shard_map(
        body, mesh=mesh, in_specs=placed, out_specs=P("gz", "theta", None), check_vma=False
    )
```

profile of v0, /device:TPU:0, one launch (start us, length us, event | category | flops | bytes accessed | tf_op | source)
XLA Modules:
  0.0 445.4 jit_solution(5071512144903572490)
XLA Ops:
  0.0 4.1 collective-permute-start.2
  4.1 1.1 fusion.91
  5.1 1.5 collective-permute-start
  6.7 62.7 %fusion.18 = f32[1024]{0:T(1024)S(1)} fusion(f32[2048]{0:T(1024)S(1)} %fusion.87, f32[1024]{0:T(1024)S(1)} %fusion.88), kind=kLoop, calls=%fused_computation.39 | loop fusion | flops 58719232 | bytes 16384 | tf_op jit(solution)/shard_map/reduce_sum | solution.py:46
  69.3 94.7 %fusion.9 = f32[1024,2048]{1,0:T(8,128)S(1)} fusion(f32[1024]{0:T(1024)S(1)} %fusion.18, f32[2048]{0:T(1024)S(1)} %fusion.87, f32[1024]{0:T(1024)S(1)} %fusion.88), kind=kLoop, calls=%fused_computation.15 | loop fusion | flops 60817408 | bytes 8404992 | tf_op jit(solution)/shard_map/sub | solution.py:46
  164.1 8.1 %fusion.23 = f32[1024,512]{0,1:T(8,128)} fusion(f32[512,1024]{1,0:T(8,128)S(1)} %bitcast.22, f32[1024,2048]{1,0:T(8,128)S(1)} %fusion.9), kind=kOutput, calls=%fused_computation.44 | convolution fusion | flops 6442450944 | bytes 8388608 | tf_op jit(solution)/shard_map/dot_general | solution.py:78
  172.2 1.5 constant_dynamic-update-slice_fusion.1
  173.7 2.2 slice.163
  175.9 34.3 %rev.3 = f32[1024,1024]{1,0:T(8,128)} reverse(f32[1024,1024]{1,0:T(8,128)} %slice.163), dimensions={1} | reverse | bytes 8388608 | tf_op jit(solution)/shard_map/rev | solution.py:48
  210.3 0.7 constant_dynamic-update-slice_fusion
  211.0 10.2 %convolution_add_fusion = f32[1024,512]{0,1:T(8,128)S(1)} fusion(f32[1024,512]{0,1:T(8,128)} %fusion.23, f32[1024,1024]{1,0:T(8,128)} %rev.3, f32[512,1024]{1,0:T(8,128)} %bitcast.1), kind=kOutput, calls=%fused_computation.127 | convolution fusion | flops 6442975232 | bytes 10485760 | tf_op jit(solution)/shard_map/dot_general | solution.py:80
  221.3 2.3 fusion.72
  223.6 1.8 collective-permute-start.5
  225.4 3.3 collective-permute-start.3
  228.7 0.4 collective-permute-start.4
  229.1 88.1 %collective-permute-done.5 = f32[8,64,1024]{2,1,0:T(8,128)S(1)} collective-permute-done((f32[8,64,1024]{2,1,0:T(8,128)S(1)}, f32[8,64,1024]{2,1,0:T(8,128)S(1)}, u32[]{:S(2)}, u32[]{:S(2)}) %collective-permute-start.5) | collective-permute-done | bytes 2097184 | tf_op jit(solution)/shard_map/ppermute | solution.py:14
  317.3 7.0 %fusion.94 = f32[512,1024]{1,0:T(8,128)S(1)} fusion(f32[512,1024]{1,0:T(8,128)S(1)} %bitcast.29, f32[1024,1024]{1,0:T(8,128)S(1)} %copy-done.1), kind=kOutput, calls=%fused_computation.142 | convolution fusion | flops 6442450944 | bytes 8388608 | tf_op jit(solution)/shard_map/dot_general | solution.py:80
  324.3 7.2 %fusion.92 = f32[512,1024]{1,0:T(8,128)S(1)} fusion(f32[512,1024]{1,0:T(8,128)S(1)} %fusion.94, f32[512,1024]{1,0:T(8,128)S(1)} %bitcast.24, f32[1024,2048]{1,0:T(8,128)S(1)} %bitcast.21), kind=kOutput, calls=%fused_computation.140 | convolution fusion | flops 6442975232 | bytes 10485760 | tf_op jit(solution)/shard_map/dot_general | solution.py:78
  331.5 2.9 fusion.54
  334.5 1.6 collective-permute-start.6
  336.1 91.0 %collective-permute-done.8 = f32[8,64,1024]{2,1,0:T(8,128)S(1)} collective-permute-done((f32[8,64,1024]{2,1,0:T(8,128)S(1)}, f32[8,64,1024]{2,1,0:T(8,128)S(1)}, u32[]{:S(2)}, u32[]{:S(2)}) %collective-permute-start.8) | collective-permute-done | bytes 2097184 | tf_op jit(solution)/shard_map/ppermute | solution.py:14
  427.1 7.0 %fusion.95 = f32[512,1024]{1,0:T(8,128)S(1)} fusion(f32[512,1024]{1,0:T(8,128)S(1)} %bitcast.28, f32[1024,1024]{1,0:T(8,128)S(1)} %copy-done.1), kind=kOutput, calls=%fused_computation.143 | convolution fusion | flops 6442450944 | bytes 8388608 | tf_op jit(solution)/shard_map/dot_general | solution.py:80
  434.1 7.2 %fusion.93 = f32[512,1024]{1,0:T(8,128)S(1)} fusion(f32[512,1024]{1,0:T(8,128)S(1)} %fusion.95, f32[512,1024]{1,0:T(8,128)S(1)} %bitcast.23, f32[1024,2048]{1,0:T(8,128)S(1)} %bitcast.21), kind=kOutput, calls=%fused_computation.141 | convolution fusion | flops 6442975232 | bytes 10485760 | tf_op jit(solution)/shard_map/dot_general | solution.py:78
  441.3 3.8 fusion.34
  (31 shorter events, 0.3 us)
Async XLA Ops:
  0.0 211.0 %collective-permute-start.2 = (f32[8,64,1024]{2,1,0:T(8,128)}, f32[8,64,1024]{2,1,0:T(8,128)}, u32[]{:S(2)}, u32[]{:S(2)}) collective-permute-start(f32[8,64,1024]{2,1,0:T(8,128)} %param.2), channel_id=1, source_target_pairs={{0,16},{2,18},{4,20},{6,22},{8,24},{10,26},{12,28},{14,30},{16,0},... | collective-permute-start | bytes 6291464 | tf_op jit(solution)/shard_map/ppermute | solution.py:14
  5.1 205.2 %collective-permute-start = (f32[8,4,1024]{2,1,0:T(4,128)S(1)}, f32[8,4,1024]{2,1,0:T(4,128)S(1)}, u32[]{:S(2)}, u32[]{:S(2)}) collective-permute-start(f32[8,4,1024]{2,1,0:T(4,128)S(1)} %get-tuple-element.9), channel_id=1, source_target_pairs={{2,0},{4,2},{6,4},{8,6},{10,8},{12,10},{14,12},{16,14},{18,16},{20... | collective-permute-start | bytes 393224 | tf_op jit(solution)/shard_map/ppermute | solution.py:25
  6.6 214.6 %collective-permute-start.1 = (f32[8,4,1024]{2,1,0:T(4,128)S(1)}, f32[8,4,1024]{2,1,0:T(4,128)S(1)}, u32[]{:S(2)}, u32[]{:S(2)}) collective-permute-start(f32[8,4,1024]{2,1,0:T(4,128)S(1)} %get-tuple-element.10), channel_id=1, source_target_pairs={{0,2},{2,4},{4,6},{6,8},{8,10},{10,12},{12,14},{14,16},{16,18},{18... | collective-permute-start | bytes 393224 | tf_op jit(solution)/shard_map/ppermute | solution.py:24
  69.3 94.8 %copy-start.2 = (f32[8,64,1024]{2,1,0:T(8,128)S(1)}, f32[8,64,1024]{2,1,0:T(8,128)}, u32[]{:S(2)}) copy-start(f32[8,64,1024]{2,1,0:T(8,128)} %param.2) | copy-start | bytes 6291460
  164.1 9.6 %copy-start = (f32[1024,2048]{1,0:T(8,128)}, f32[1024,2048]{1,0:T(8,128)S(1)}, u32[]{:S(2)}) copy-start(f32[1024,2048]{1,0:T(8,128)S(1)} %fusion.9) | copy-start | bytes 25165828
  175.9 34.3 %copy-start.4 = (f32[1024]{0:T(1024)S(1)}, f32[1024]{0:T(1024)}, u32[]{:S(2)}) copy-start(f32[1024]{0:T(1024)} %param.3) | copy-start | bytes 12292
  211.0 10.3 %copy-start.3 = (f32[8,68,1024]{2,1,0:T(8,128)S(1)}, f32[8,68,1024]{2,1,0:T(8,128)}, u32[]{:S(2)}) copy-start(f32[8,68,1024]{2,1,0:T(8,128)} %constant_dynamic-update-slice_fusion) | copy-start | bytes 6684676
  211.0 113.2 %slice-start = ((s8[8388608]{0:T(1024)(128)(4,1)}), s8[4194304]{0:T(1024)(128)(4,1)S(1)}, s32[]{:S(2)}) async-start(s8[8388608]{0:T(1024)(128)(4,1)} %bitcast.20), calls=%async_computation | async-start | bytes 8388608
  221.3 96.0 %copy-start.1 = (f32[1024,1024]{1,0:T(8,128)S(1)}, f32[1024,1024]{1,0:T(8,128)}, u32[]{:S(2)}) copy-start(f32[1024,1024]{1,0:T(8,128)} %rev.3) | copy-start | bytes 12582916
  221.3 103.0 %slice-start.1 = ((s8[8388608]{0:T(1024)(128)(4,1)}), s8[4194304]{0:T(1024)(128)(4,1)S(1)}, s32[]{:S(2)}) async-start(s8[8388608]{0:T(1024)(128)(4,1)} %bitcast.20), calls=%async_computation.1 | async-start | bytes 8388608
  223.6 93.7 %collective-permute-start.5 = (f32[8,64,1024]{2,1,0:T(8,128)S(1)}, f32[8,64,1024]{2,1,0:T(8,128)S(1)}, u32[]{:S(2)}, u32[]{:S(2)}) collective-permute-start(f32[8,64,1024]{2,1,0:T(8,128)S(1)} %fusion.72), channel_id=1, source_target_pairs={{0,16},{2,18},{4,20},{6,22},{8,24},{10,26},{12,28},{14,30},{16,0},... | collective-permute-start | bytes 6291464 | tf_op jit(solution)/shard_map/ppermute | solution.py:14
  225.4 106.0 %collective-permute-start.3 = (f32[8,4,1024]{2,1,0:T(4,128)S(1)}, f32[8,4,1024]{2,1,0:T(4,128)S(1)}, u32[]{:S(2)}, u32[]{:S(2)}) collective-permute-start(f32[8,4,1024]{2,1,0:T(4,128)S(1)} %get-tuple-element.7), channel_id=1, source_target_pairs={{2,0},{4,2},{6,4},{8,6},{10,8},{12,10},{14,12},{16,14},{18,16},{20... | collective-permute-start | bytes 393224 | tf_op jit(solution)/shard_map/ppermute | solution.py:25
  228.7 102.7 %collective-permute-start.4 = (f32[8,4,1024]{2,1,0:T(4,128)S(1)}, f32[8,4,1024]{2,1,0:T(4,128)S(1)}, u32[]{:S(2)}, u32[]{:S(2)}) collective-permute-start(f32[8,4,1024]{2,1,0:T(4,128)S(1)} %get-tuple-element.8), channel_id=1, source_target_pairs={{0,2},{2,4},{4,6},{6,8},{8,10},{10,12},{12,14},{14,16},{16,18},{18... | collective-permute-start | bytes 393224 | tf_op jit(solution)/shard_map/ppermute | solution.py:24
  334.3 92.8 %collective-permute-start.8 = (f32[8,64,1024]{2,1,0:T(8,128)S(1)}, f32[8,64,1024]{2,1,0:T(8,128)S(1)}, u32[]{:S(2)}, u32[]{:S(2)}) collective-permute-start(f32[8,64,1024]{2,1,0:T(8,128)S(1)} %fusion.54), channel_id=1, source_target_pairs={{0,16},{2,18},{4,20},{6,22},{8,24},{10,26},{12,28},{14,30},{16,0},... | collective-permute-start | bytes 6291464 | tf_op jit(solution)/shard_map/ppermute | solution.py:14
  334.5 106.8 %collective-permute-start.6 = (f32[8,4,1024]{2,1,0:T(4,128)S(1)}, f32[8,4,1024]{2,1,0:T(4,128)S(1)}, u32[]{:S(2)}, u32[]{:S(2)}) collective-permute-start(f32[8,4,1024]{2,1,0:T(4,128)S(1)} %get-tuple-element.5), channel_id=1, source_target_pairs={{2,0},{4,2},{6,4},{8,6},{10,8},{12,10},{14,12},{16,14},{18,16},{20... | collective-permute-start | bytes 393224 | tf_op jit(solution)/shard_map/ppermute | solution.py:25
  336.1 105.2 %collective-permute-start.7 = (f32[8,4,1024]{2,1,0:T(4,128)S(1)}, f32[8,4,1024]{2,1,0:T(4,128)S(1)}, u32[]{:S(2)}, u32[]{:S(2)}) collective-permute-start(f32[8,4,1024]{2,1,0:T(4,128)S(1)} %get-tuple-element.6), channel_id=1, source_target_pairs={{0,2},{2,4},{4,6},{6,8},{8,10},{10,12},{12,14},{14,16},{16,18},{18... | collective-permute-start | bytes 393224 | tf_op jit(solution)/shard_map/ppermute | solution.py:24
where the time goes:
time: 454 us; the launch traced here: 445 us
  waiting for transfers between devices  179 us (39%)
  other arithmetic  166 us (37%)
  matrix products  46.6 us (10%)
  local copies, waits for them, and re-layouts  39.9 us (9%)
  starting transfers between devices  12.7 us (3%)
    ppermute x3, waiting for transfers between devices, shifted(): return lax.ppermute(x, axis, [(i, (i + by) % size) for i in range(size)])  179 us
    sub x1, other arithmetic, diameter_blocks(): offdiag - jnp.where(same, jnp.sum(offdiag, axis=1, keepdims=True), 0.0)  94.7 us
    reduce_sum x1, other arithmetic, diameter_blocks(): jnp.sum(offdiag, axis=1, keepdims=True)  62.7 us
    rev x1, local copies, waits for them, and re-layouts, diameter_blocks(): far = matrix[:, radial_count:][:, ::-1].T  34.3 us
    dot_general x3, matrix products, opposite_derivative(): jnp.dot(other.reshape(-1, radial_count), far, precision=lax.Precision.HIG...  24.1 us
    dot_general x3, matrix products, opposite_derivative(): local_part = jnp.dot(own_rows, near, precision=lax.Precision.HIGHEST)  22.5 us
  transfers between devices with their start and end apart: 9, of which 2 were waited for; matrix products, arithmetic and copies ran while one was open for 55% of the time, Pallas kernels for 0%

commit v1 on v0

v1 whole, which is shorter than its diff:
```python
import functools

import jax
import jax.numpy as jnp
import numpy as np
from jax import lax
from jax.experimental import pallas as pl
from jax.experimental.pallas import tpu as pltpu
from jax.sharding import PartitionSpec as P

stencil_weights = (4.0 / 5.0, -1.0 / 5.0, 4.0 / 105.0, -1.0 / 280.0)
radial_step = 0.2
PLANES = 4
PAD = 8
TILE = 256
MESH = pl.DeviceIdType.MESH


def radial_tables(radial_count):
    last = 2 * radial_count - 1
    i = np.arange(radial_count)
    l = np.arange(last + 1)
    unit = np.pi / (2 * last)
    x = np.cos(2 * unit * i)
    high = x.astype(np.float32)
    low = (x - high.astype(np.float64)).astype(np.float32)
    gap = -2.0 * np.sin(unit * (i[:, None] + l)) * np.sin(unit * (i[:, None] - l))
    same = i[:, None] == l
    ci = np.where(i == 0, 2.0, 1.0)
    cl = np.where((l == 0) | (l == last), 2.0, 1.0)
    sign = np.where((i[:, None] + l) % 2 == 0, 1.0, -1.0)
    off = np.where(same, 0.0, ci[:, None] / cl * sign / np.where(same, 1.0, gap))
    diagonal = -off.sum(axis=1)
    mirror = off[i, last - i]
    scale = 0.5 * radial_step / last * np.sin(2 * unit * i) ** 2
    column = scale * ci * np.where(i % 2 == 0, 1.0, -1.0)
    row = np.where(i % 2 == 0, 1.0, -1.0) / ci
    even = scale * (diagonal + mirror)
    odd = scale * (diagonal - mirror)
    return np.stack([high, low, column, row, even, odd, 0 * x, 0 * x]).astype(np.float32)


def build_matrices(table, mats, radial_count):
    blk = 128

    @pl.loop(0, radial_count // blk)
    def _(lb):
        l0 = pl.multiple_of(lb * blk, blk)

        def down(k):
            return jnp.transpose(jnp.broadcast_to(table[k : k + 1, pl.ds(l0, blk)], (blk, blk)))

        high, low, row = down(0), down(1), down(3)
        rows = lax.broadcasted_iota(jnp.int32, (blk, blk), 0) + l0

        @pl.loop(0, radial_count // blk)
        def _(jb):
            j0 = pl.multiple_of(jb * blk, blk)
            cols = pl.ds(j0, blk)
            same = rows == lax.broadcasted_iota(jnp.int32, (blk, blk), 1) + j0
            near = (table[0:1, cols] - high) + (table[1:2, cols] - low)
            far = table[0:1, cols] + high
            near = 1.0 / jnp.where(same, 1.0, near)
            far = 1.0 / far
            factor = table[2:3, cols] * row
            even = jnp.where(same, table[4:5, cols], factor * (near - far))
            odd = jnp.where(same, table[5:6, cols], factor * (near + far))
            for k, m in enumerate((even, odd)):
                head = m.astype(jnp.bfloat16)
                mats[2 * k, pl.ds(l0, blk), cols] = head
                mats[2 * k + 1, pl.ds(l0, blk), cols] = (m - head.astype(jnp.float32)).astype(jnp.bfloat16)


def kernel(
    size,
    field,
    courant,
    table,
    out,
    state,
    mats,
    split,
    deriv,
    edge_out,
    edge_in,
    own_sem,
    in_send,
    in_recv,
    out_send,
    out_recv,
    edge_send,
    edge_recv,
):
    ring = size // PLANES
    heights, rows, radial_count = field.shape
    per = heights // PLANES
    half = PLANES // 2
    me = lax.axis_index("theta")
    g = lax.div(me, ring)
    q = lax.rem(me, ring)
    right = g * ring + lax.rem(q + 1, ring)
    left = g * ring + lax.rem(q + ring - 1, ring)
    high_bit, low_bit = lax.div(g, 2), lax.rem(g, 2)

    def partner(m):
        a, b = m // 2, m % 2
        return 2 * (high_bit + a - 2 * a * high_bit) + (low_bit + b - 2 * b * low_bit)

    order = (3, 2, 1)
    others = [partner(m) for m in order]
    body = pl.ds(PAD, rows)

    barrier = pltpu.get_barrier_semaphore()
    for d in [o * ring + q for o in others] + [right, left]:
        pl.semaphore_signal(barrier, inc=1, device_id={"theta": d}, device_id_type=MESH)
    pl.semaphore_wait(barrier, len(others) + 2)

    def incoming(h, k):
        o = others[k]
        return pltpu.make_async_remote_copy(
            field.at[o * per + h],
            state.at[0, h, g, body],
            in_send.at[h, k],
            in_recv.at[h, k],
            device_id={"theta": o * ring + q},
            device_id_type=MESH,
        )

    def outgoing(h, k):
        o = others[k]
        return pltpu.make_async_remote_copy(
            state.at[3, h, o, body],
            out.at[g * per + h],
            out_send.at[h, k],
            out_recv.at[h, k],
            device_id={"theta": o * ring + q},
            device_id_type=MESH,
        )

    def own_in(h):
        return pltpu.make_async_copy(field.at[g * per + h], state.at[0, h, g, body], own_sem.at[0, h])

    def own_out(h):
        return pltpu.make_async_copy(state.at[3, h, g, body], out.at[g * per + h], own_sem.at[1, h])

    def edge(sec, h, way):
        return pltpu.make_async_remote_copy(
            edge_out.at[sec, h, way],
            edge_in.at[sec, h, way],
            edge_send.at[sec, h, way],
            edge_recv.at[sec, h, way],
            device_id={"theta": right if way == 0 else left},
            device_id_type=MESH,
        )

    for h in range(per):
        for k in range(len(order)):
            incoming(h, k).start()
        own_in(h).start()

    build_matrices(table, mats, radial_count)

    wrap_right = lax.div(q, ring - 1)
    wrap_left = lax.div(ring - 1 - q, ring - 1)
    pair_rows = half * rows
    tiles = radial_count // TILE

    @pl.loop(0, per * 3)
    def _(step):
        h = lax.div(step, 3)
        sec = lax.rem(step, 3)

        @pl.when(sec == 0)
        def _():
            own_in(h).wait()
            for k in range(len(order)):
                incoming(h, k).wait_recv()

        for s in range(PLANES):
            src = lax.rem(s + PLANES - wrap_right, PLANES)
            edge_out[sec, h, 0, 4 * s : 4 * s + 4] = state[sec, h, src, PAD + rows - 4 : PAD + rows]
            src = lax.rem(s + wrap_left, PLANES)
            edge_out[sec, h, 1, 4 * s : 4 * s + 4] = state[sec, h, src, PAD : PAD + 4]
        edge(sec, h, 0).start()
        edge(sec, h, 1).start()

        @pl.loop(0, tiles)
        def _(c):
            cols = pl.ds(pl.multiple_of(c * TILE, TILE), TILE)
            for s in range(half):
                a = state[sec, h, s, body, cols]
                b = state[sec, h, s + half, body, cols]
                for k, w in enumerate((a + b, a - b)):
                    head = w.astype(jnp.bfloat16)
                    tail = (w - head.astype(jnp.float32)).astype(jnp.bfloat16)
                    split[k, s * rows : (s + 1) * rows, cols] = head
                    split[k, pair_rows + s * rows : pair_rows + (s + 1) * rows, cols] = tail

        @pl.loop(0, tiles)
        def _(c):
            cols = pl.ds(pl.multiple_of(c * TILE, TILE), TILE)
            parts = []
            for k in range(2):
                both = jnp.dot(split[k], mats[2 * k, :, cols], preferred_element_type=jnp.float32)
                rest = jnp.dot(
                    split[k, :pair_rows], mats[2 * k + 1, :, cols], preferred_element_type=jnp.float32
                )
                parts.append(both[:pair_rows] + (both[pair_rows:] + rest))
            deriv[0, :, cols] = parts[0] + parts[1]
            deriv[1, :, cols] = parts[0] - parts[1]

        edge(sec, h, 0).wait()
        edge(sec, h, 1).wait()
        for s in range(PLANES):
            state[sec, h, s, PAD - 4 : PAD] = edge_in[sec, h, 0, 4 * s : 4 * s + 4]
            state[sec, h, s, PAD + rows : PAD + rows + 4] = edge_in[sec, h, 1, 4 * s : 4 * s + 4]

        start_part = jnp.where(sec == 0, 0.0, jnp.where(sec == 1, 0.75, 1.0 / 3.0)).astype(jnp.float32)
        step_part = jnp.where(sec == 0, 1.0, jnp.where(sec == 1, 0.25, 2.0 / 3.0)).astype(jnp.float32)

        @pl.loop(0, tiles)
        def _(c):
            cols = pl.ds(pl.multiple_of(c * TILE, TILE), TILE)
            speed = courant[:, cols]
            for s in range(PLANES):
                total = jnp.zeros((rows, TILE), jnp.float32)
                for o in range(1, 5):
                    total = total + stencil_weights[o - 1] * (
                        state[sec, h, s, PAD + o : PAD + o + rows, cols]
                        - state[sec, h, s, PAD - o : PAD - o + rows, cols]
                    )
                now = state[sec, h, s, body, cols]
                d = deriv[s // half, (s % half) * rows : (s % half + 1) * rows, cols]
                moved = now - speed * total - now * d
                state[sec + 1, h, s, body, cols] = start_part * state[0, h, s, body, cols] + step_part * moved

        @pl.when(sec == 2)
        def _():
            for k in range(len(order)):
                outgoing(h, k).start()
            own_out(h).start()

    for h in range(per):
        for k in range(len(order)):
            incoming(h, k).wait_send()
        own_out(h).wait()
    for h in range(per):
        for k in range(len(order)):
            outgoing(h, k).wait()


def body(size, field, courant):
    heights, rows, radial_count = field.shape
    per = heights // PLANES
    table = jnp.asarray(radial_tables(radial_count))
    f32, bf16 = jnp.float32, jnp.bfloat16
    dma = pltpu.SemaphoreType.DMA
    vmem = pl.BlockSpec(memory_space=pltpu.VMEM)
    anywhere = pl.BlockSpec(memory_space=pl.ANY)
    return pl.pallas_call(
        functools.partial(kernel, size),
        out_shape=jax.ShapeDtypeStruct(field.shape, f32),
        in_specs=[anywhere, vmem, vmem],
        out_specs=anywhere,
        scratch_shapes=[
            pltpu.VMEM((4, per, PLANES, rows + 2 * PAD, radial_count), f32),
            pltpu.VMEM((4, radial_count, radial_count), bf16),
            pltpu.VMEM((2, PLANES * rows, radial_count), bf16),
            pltpu.VMEM((2, PLANES // 2 * rows, radial_count), f32),
            pltpu.VMEM((3, per, 2, 4 * PLANES, radial_count), f32),
            pltpu.VMEM((3, per, 2, 4 * PLANES, radial_count), f32),
            dma((2, per)),
            dma((per, PLANES - 1)),
            dma((per, PLANES - 1)),
            dma((per, PLANES - 1)),
            dma((per, PLANES - 1)),
            dma((3, per, 2)),
            dma((3, per, 2)),
        ],
        compiler_params=pltpu.CompilerParams(
            collective_id=0, has_side_effects=True, vmem_limit_bytes=56 << 20
        ),
    )(field, courant.reshape(1, -1), table)


def solution(mesh):
    size = mesh.shape["theta"]
    return jax.shard_map(
        functools.partial(body, size),
        mesh=mesh,
        in_specs=(P("gz", "theta", None), P()),
        out_specs=P("gz", "theta", None),
        check_vma=False,
    )
```

time: 454 us -> 101 us (0.22); the launches traced: 445 us -> 101 us
  waiting for transfers between devices: 179 us -> 0 us
  other arithmetic: 166 us -> 0 us
  Pallas kernels: 0 us -> 98 us
  matrix products: 46.6 us -> 0 us
  local copies, waits for them, and re-layouts: 39.9 us -> 3.16 us
  starting transfers between devices: 12.7 us -> 0 us
    ppermute x9 -> x0, waiting for transfers between devices: 179 us -> none  [the longest x3 179 us: shifted(): return lax.ppermute(x, axis, [(i, (i + by) % size) for i in range(size)])]
    pallas_call x0 -> x1, Pallas kernels: none -> 98 us  [body(): pl.pallas_call(functools.partial(kernel, size), out_shape=jax.ShapeDtypeS...]
    sub x1 -> x0, other arithmetic: 94.7 us -> none  [diameter_blocks(): offdiag - jnp.where(same, jnp.sum(offdiag, axis=1, keepdims=True), 0.0)]
    reduce_sum x1 -> x0, other arithmetic: 62.7 us -> none  [diameter_blocks(): jnp.sum(offdiag, axis=1, keepdims=True)]
    dot_general x6 -> x0, matrix products: 46.6 us -> none  [the longest x3 24.1 us: opposite_derivative(): jnp.dot(other.reshape(-1, radial_count), far, precision=lax.Precision.HIG...]
    rev x1 -> x0, local copies, waits for them, and re-layouts: 34.3 us -> none  [diameter_blocks(): far = matrix[:, radial_count:][:, ::-1].T]
    ppermute x9 -> x0, starting transfers between devices: 12.7 us -> none  [the longest x3 6.44 us: with_halo(): after = lax.ppermute(leading, axis, down)]
    add x3 -> x0, other arithmetic: 9.01 us -> none  [the longest x1 3.83 us: body(): return field / 3.0 + 2.0 / 3.0 * (second + section_rate(widen(second)))]
  transfers between devices with their start and end apart: 9 -> 0, of which waited for: 2 -> 0; matrix products, arithmetic and copies ran while one was open for 55% -> 0% of each run, Pallas kernels for 0% -> 0%
where the time goes in v1:
time: 101 us
  Pallas kernels  98 us (97%)
  local copies, waits for them, and re-layouts  3.16 us (3%)
    pallas_call x1, Pallas kernels, body(): pl.pallas_call(functools.partial(kernel, size), out_shape=jax.ShapeDtypeS...  98 us
    unnamed x1, local copies, waits for them, and re-layouts  3.16 us

profile of v1, /device:TPU:0, one launch (start us, length us, event | category | flops | bytes accessed | tf_op | source)
XLA Modules:
  0.0 101.2 jit_solution(14294424008255925846)
XLA Ops:
  0.0 98.0 %shard_map.37 = f32[8,64,1024]{2,1,0:T(8,128)} custom-call(f32[8,64,1024]{2,1,0:T(8,128)} %field.1, f32[1,1024]{1,0:T(1,128)} %bitcast.1, f32[8,1024]{1,0:T(8,128)} %constant.2.clone.table), custom_call_target="tpu_custom_call" | custom-call | tf_op jit(solution)/shard_map/pallas_call | solution.py:260
  98.0 3.2 %copy.5 = f32[8,64,1024]{2,1,0:T(8,128)} copy(f32[8,64,1024]{2,1,0:T(8,128)} %shard_map.37) | data formatting | bytes 4194304

commit v2 on v1

--- a/solution.py
+++ b/solution.py
@@ -74,15 +74,18 @@
 def kernel(
     size,
     field,
+    courant_in,
+    table_in,
+    out,
     courant,
     table,
-    out,
     state,
     mats,
     split,
     deriv,
     edge_out,
     edge_in,
+    table_sem,
     own_sem,
     in_send,
     in_recv,
@@ -158,6 +161,14 @@
             incoming(h, k).start()
         own_in(h).start()
 
+    loads = [
+        pltpu.make_async_copy(table_in, table, table_sem.at[0]),
+        pltpu.make_async_copy(courant_in, courant, table_sem.at[1]),
+    ]
+    for load in loads:
+        load.start()
+    for load in loads:
+        load.wait()
     build_matrices(table, mats, radial_count)
 
     wrap_right = lax.div(q, ring - 1)
@@ -236,7 +247,7 @@
 
         @pl.when(sec == 2)
         def _():
-            for k in range(len(order)):
+            for k in (1, 2, 0):
                 outgoing(h, k).start()
             own_out(h).start()
 
@@ -255,20 +266,22 @@
     table = jnp.asarray(radial_tables(radial_count))
     f32, bf16 = jnp.float32, jnp.bfloat16
     dma = pltpu.SemaphoreType.DMA
-    vmem = pl.BlockSpec(memory_space=pltpu.VMEM)
     anywhere = pl.BlockSpec(memory_space=pl.ANY)
     return pl.pallas_call(
         functools.partial(kernel, size),
-        out_shape=jax.ShapeDtypeStruct(field.shape, f32),
-        in_specs=[anywhere, vmem, vmem],
-        out_specs=anywhere,
+        out_shape=pltpu.VMEM(field.shape, f32),
+        in_specs=[anywhere] * 3,
+        out_specs=pl.BlockSpec(memory_space=pltpu.VMEM),
         scratch_shapes=[
+            pltpu.VMEM((1, radial_count), f32),
+            pltpu.VMEM(table.shape, f32),
             pltpu.VMEM((4, per, PLANES, rows + 2 * PAD, radial_count), f32),
             pltpu.VMEM((4, radial_count, radial_count), bf16),
             pltpu.VMEM((2, PLANES * rows, radial_count), bf16),
             pltpu.VMEM((2, PLANES // 2 * rows, radial_count), f32),
             pltpu.VMEM((3, per, 2, 4 * PLANES, radial_count), f32),
             pltpu.VMEM((3, per, 2, 4 * PLANES, radial_count), f32),
+            dma((2,)),
             dma((2, per)),
             dma((per, PLANES - 1)),
             dma((per, PLANES - 1)),
@@ -278,9 +291,9 @@
             dma((3, per, 2)),
         ],
         compiler_params=pltpu.CompilerParams(
-            collective_id=0, has_side_effects=True, vmem_limit_bytes=56 << 20
+            collective_id=0, has_side_effects=True, vmem_limit_bytes=40 << 20
         ),
-    )(field, courant.reshape(1, -1), table)
+    )(*[pltpu.with_memory_space_constraint(x, pltpu.HBM) for x in (field, courant.reshape(1, -1), table)])
 
 
 def solution(mesh):

time: 101 us -> 96.1 us (0.951)
  the two profiles are of different devices: /device:TPU:0 before, /device:TPU:8 now
where the time goes in v2:
time: 96.1 us; the launch traced here: 96 us
  Pallas kernels  94.7 us (99%)
  local copies, waits for them, and re-layouts  1.32 us (1%)
    pallas_call x1, Pallas kernels, body(): pl.pallas_call(functools.partial(kernel, size), out_shape=pltpu.VMEM(fiel...  94.7 us

profile of v2, /device:TPU:8, one launch (start us, length us, event | category | flops | bytes accessed | tf_op | source)
XLA Modules:
  0.0 96.0 jit_solution(1161552554907662644)
XLA Ops:
  0.0 94.7 %shard_map.37 = f32[8,64,1024]{2,1,0:T(8,128)S(1)} custom-call(f32[8,64,1024]{2,1,0:T(8,128)} %field.1, f32[1,1024]{1,0:T(1,128)} %bitcast.1, f32[8,1024]{1,0:T(8,128)} %constant.2.clone.table_in), custom_call_target="tpu_custom_call" | custom-call | tf_op jit(solution)/shard_map/pallas_call | solution.py:270
  94.7 1.3 %copy.5 = f32[8,64,1024]{2,1,0:T(8,128)} copy(f32[8,64,1024]{2,1,0:T(8,128)S(1)} %shard_map.37) | data formatting | bytes 4194304
